TPU v7x, 256 devices: a whole 4x4x8 slice. The times are simulated.
256 devices in a mesh: dp: 2 (over core), seq: 16 (over x, y), tensor: 8 (over z).
Axes of the slice: x: 4, y: 4, z: 8, core: 2. Of those that a mesh axis runs over, the one named last changes fastest.
Arguments:
- hidden: bfloat16 [16384, 7168], P(('dp', 'seq')), may hold values from -34 to 34
- grad_out: bfloat16 [16384, 4096], P(('dp', 'seq'), 'tensor'), may hold values from -24 to 24
- master_weight: float32 [7168, 4096], P(('dp', 'seq'), 'tensor'), may hold values from -6 to 6
- row_prev: float32 [7168], P(('dp', 'seq')), may hold values from 0.01 to 0.3
- col_prev: float32 [4096], P('tensor'), may hold values from 0.01 to 0.3
Outputs:
- new_weight: bfloat16 [7168, 4096], P('dp', 'tensor')
- update: float32 [7168, 4096], P(('dp', 'seq'), 'tensor')
- new_rows: float32 [7168], P(('dp', 'seq'))
- new_cols: float32 [4096], P('tensor')
All inputs are finite; a program needn't handle non-finite values.
Results may differ from a plain program's by a relative error of at most 0.0004.
Values may be sent and summed in bfloat16 or wider, within the bound.
A program may use at most 128 MiB of HBM per device.

v0:
```python
import jax
import jax.numpy as jnp
from jax import lax
from jax.sharding import PartitionSpec as P

D = 4096
FF_WIN = 7168
decay_rate = 0.8
learn_rate = 0.05
small_term = 1e-06


def per_device(hidden, grad_out, master_weight, row_prev, col_prev):
    grads = lax.psum_scatter(
        lax.dot_general(
            hidden, grad_out, (((0,), (0,)), ((), ())), preferred_element_type=jnp.float32
        ),
        ("dp", "seq"),
        scatter_dimension=0,
        tiled=True,
    )
    squares = grads * grads + small_term
    col_total = lax.psum(jnp.sum(squares, axis=0), ("dp", "seq"))
    row_total = lax.psum(jnp.sum(squares, axis=1), "tensor")
    new_rows = decay_rate * row_prev + (1.0 - decay_rate) * row_total / D
    new_cols = decay_rate * col_prev + (1.0 - decay_rate) * col_total / FF_WIN
    second = new_rows[:, None] * new_cols[None, :]
    raw = grads / jnp.sqrt(second)
    raw_total = lax.psum(jnp.sum(raw * raw), ("dp", "seq", "tensor"))
    size = jnp.sqrt(raw_total / (FF_WIN * D))
    update = raw / jnp.maximum(1.0, size)
    fresh = (master_weight - learn_rate * update).astype(jnp.bfloat16)
    new_weight = lax.all_gather(fresh, "seq", axis=0, tiled=True)
    return (new_weight, update, new_rows, new_cols)


def solution(mesh):
    return jax.shard_map(
        per_device,
        mesh=mesh,
        in_specs=(
            P(("dp", "seq"), None),
            P(("dp", "seq"), "tensor"),
            P(("dp", "seq"), "tensor"),
            P(("dp", "seq")),
            P("tensor"),
        ),
        out_specs=(P("dp", "tensor"), P(("dp", "seq"), "tensor"), P(("dp", "seq")), P("tensor")),
        check_vma=False,
    )
```

profile of v0, /device:TPU:1, one launch (start us, length us, event | category | flops | bytes accessed | tf_op | source)
XLA Modules:
  0.0 362.4 jit_solution(1551394529505662)
XLA Ops:
  7.2 0.0 copy-start
  7.2 0.0 reduce-scatter.2.cloned.1.call-start
  7.2 1.0 copy-done
  8.2 10.5 %fusion.4 = f32[7168,512]{1,0:T(8,128)} fusion(bf16[512,7168]{1,0:T(8,128)(2,1)} %param.5, bf16[512,512]{1,0:T(8,128)(2,1)S(1)} %copy-done), kind=kOutput, calls=%fused_computation.9 | convolution fusion | flops 3758096384 | bytes 22544384 | tf_op jit(solution)/shard_map/dot_general | solution.py:15
  18.7 0.0 copy-start.5
  18.7 0.0 copy-start.4
  18.7 0.0 copy-start.1
  18.7 0.0 reduce-scatter.2.cloned.1.call-update
  18.7 0.0 all-gather.2.cloned.1.call-start
  18.8 120.1 %reduce-scatter.2.cloned.1.call-done = f32[224,512]{1,0:T(8,128)} async-done(((f32[7168,512]{1,0:T(8,128)}), f32[224,512]{1,0:T(8,128)}) %reduce-scatter.2.cloned.1.call-update) | async-done | bytes 458768 | tf_op jit(solution)/shard_map/reduce_scatter | solution.py:14
  138.9 1.2 fusion.1
  140.0 13.7 %psum.21 = f32[224]{0:T(256)S(1)} all-reduce(f32[224]{0:T(256)S(1)} %get-tuple-element.4), channel_id=1, replica_groups=mesh['dp'=2,'seq'=16,'tensor'=8] {'tensor'}, use_global_device_ids=true, to_apply=%region_2.0 | all-reduce | flops 224 | bytes 1792 | tf_op jit(solution)/shard_map/psum | solution.py:24
  153.8 70.5 %psum.22 = f32[512]{0:T(512)S(1)} all-reduce(f32[512]{0:T(512)S(1)} %get-tuple-element.5), channel_id=1, replica_groups=mesh['dp'=2,'seq'=16,'tensor'=8] {'dp','seq'}, use_global_device_ids=true, to_apply=%region_4.0 | all-reduce | flops 512 | bytes 4096 | tf_op jit(solution)/shard_map/psum | solution.py:23
  224.3 0.0 copy-done.5
  224.3 0.0 copy-done.4
  224.3 0.0 copy-start.3
  224.4 0.0 copy-start.2
  224.4 1.8 multiply_reduce_fusion
  226.2 72.1 %psum.23 = f32[]{:T(128)} all-reduce(f32[]{:T(128)} %multiply_reduce_fusion), channel_id=1, replica_groups=mesh['dp'=2,'seq'=16,'tensor'=8] {'dp','seq','tensor'}, use_global_device_ids=true, to_apply=%region_6.0 | all-reduce | flops 1 | bytes 8 | tf_op jit(solution)/shard_map/psum | solution.py:29
  299.0 0.0 copy-done.1
  299.0 2.0 subtract_convert_fusion
  301.0 0.0 all-gather.2.cloned.1.call-update
  301.1 50.3 %all-gather.2.cloned.1.call-done = bf16[3584,512]{1,0:T(8,128)(2,1)} async-done(((bf16[224,512]{1,0:T(8,128)(2,1)}), bf16[3584,512]{1,0:T(8,128)(2,1)}) %all-gather.2.cloned.1.call-update) | async-done | bytes 3670032 | tf_op jit(solution)/shard_map/all_gather | solution.py:33
  351.4 4.1 %copy.10 = bf16[3584,512]{1,0:T(8,128)(2,1)} copy(bf16[3584,512]{1,0:T(8,128)(2,1)} %all-gather.2.cloned.1.call-done) | data formatting | bytes 7340032
  355.5 0.0 copy-done.3
  355.5 0.0 copy-done.2
  (2 shorter events, 0.0 us)
Async XLA Ops:
  7.2 1.0 copy-start
  7.2 131.7 %reduce-scatter.2.cloned.1.call-start = ((), (), s32[]{:S(2)}) async-start(), calls=%async_computation.1 | async-start | bytes 15138816 | tf_op jit(solution)/shard_map/reduce_scatter | solution.py:14
  18.7 205.6 %copy-start.5 = (f32[224]{0:T(256)S(1)}, f32[224]{0:T(256)}, u32[]{:S(2)}) copy-start(f32[224]{0:T(256)} %param.8) | copy-start | bytes 2692
  18.7 205.6 %copy-start.4 = (f32[512]{0:T(512)S(1)}, f32[512]{0:T(512)}, u32[]{:S(2)}) copy-start(f32[512]{0:T(512)} %param.9) | copy-start | bytes 6148
  18.7 280.3 %copy-start.1 = (f32[224,512]{1,0:T(8,128)S(1)}, f32[224,512]{1,0:T(8,128)}, u32[]{:S(2)}) copy-start(f32[224,512]{1,0:T(8,128)} %param.7) | copy-start | bytes 1376260
  18.7 332.7 %all-gather.2.cloned.1.call-start = ((), (), s32[]{:S(2)}) async-start(), calls=%async_computation.2 | async-start | bytes 3899392 | tf_op jit(solution)/shard_map/all_gather | solution.py:33
  224.3 131.2 %copy-start.3 = (f32[224]{0:T(256)}, f32[224]{0:T(256)S(1)}, u32[]{:S(2)}) copy-start(f32[224]{0:T(256)S(1)} %multiply_add_fusion.2) | copy-start | bytes 2692
  224.4 131.1 %copy-start.2 = (f32[512]{0:T(512)}, f32[512]{0:T(512)S(1)}, u32[]{:S(2)}) copy-start(f32[512]{0:T(512)S(1)} %multiply_add_fusion.1) | copy-start | bytes 6148
Sparse Core Ops, SparseCore 0:
  18.8 119.9 reduce-scatter.1
  301.2 50.1 all-gather.1
where the time goes:
time: 363 us; the launch traced here: 362 us
  waiting for transfers between devices  170 us (47%)
  blocking collectives  156 us (43%)
  between operations  14.8 us (4%)
  matrix products  10.5 us (3%)
  local copies, waits for them, and re-layouts  5.13 us (1%)
  other arithmetic  5.03 us (1%)
    reduce_scatter x1, waiting for transfers between devices, per_device(): lax.psum_scatter(lax.dot_general(hidden, grad_out, (((0,), (0,)), ((), ()...  120 us
    psum x1, blocking collectives, per_device(): raw_total = lax.psum(jnp.sum(raw * raw), ('dp', 'seq', 'tensor'))  72.1 us
    psum x1, blocking collectives, per_device(): col_total = lax.psum(jnp.sum(squares, axis=0), ('dp', 'seq'))  70.5 us
    all_gather x1, waiting for transfers between devices, per_device(): new_weight = lax.all_gather(fresh, 'seq', axis=0, tiled=True)  50.3 us
    psum x1, blocking collectives, per_device(): row_total = lax.psum(jnp.sum(squares, axis=1), 'tensor')  13.7 us
    dot_general x1, matrix products, per_device(): lax.dot_general(hidden, grad_out, (((0,), (0,)), ((), ())), preferred_ele...  10.5 us
  transfers between devices with their start and end apart: 2, of which 2 were waited for; matrix products, arithmetic and copies ran while one was open for 0% of the time, Pallas kernels for 0%

commit v1 on v0

--- a/solution.py
+++ b/solution.py
@@ -21,7 +21,9 @@
     )
     squares = grads * grads + small_term
     col_total = lax.psum(jnp.sum(squares, axis=0), ("dp", "seq"))
-    row_total = lax.psum(jnp.sum(squares, axis=1), "tensor")
+    own = jnp.sum(squares, axis=1)
+    parts = lax.all_gather(own, "tensor")
+    row_total = jnp.sum(parts, axis=0)
     new_rows = decay_rate * row_prev + (1.0 - decay_rate) * row_total / D
     new_cols = decay_rate * col_prev + (1.0 - decay_rate) * col_total / FF_WIN
     second = new_rows[:, None] * new_cols[None, :]

time: 363 us -> 363 us (level)
    unnamed x0 -> x1, blocking collectives: none -> 13.9 us
    psum x1 -> x0, blocking collectives: 13.7 us -> none  [per_device(): row_total = lax.psum(jnp.sum(squares, axis=1), 'tensor')]
where the time goes in v1:
time: 363 us
  waiting for transfers between devices  169 us (47%)
  blocking collectives  157 us (43%)
  between operations  15.5 us (4%)
  matrix products  10.5 us (3%)
  local copies, waits for them, and re-layouts  6.65 us (2%)
  other arithmetic  5.06 us (1%)
    reduce_scatter x1, waiting for transfers between devices, per_device(): lax.psum_scatter(lax.dot_general(hidden, grad_out, (((0,), (0,)), ((), ()...  118 us
    psum x1, blocking collectives, per_device(): raw_total = lax.psum(jnp.sum(raw * raw), ('dp', 'seq', 'tensor'))  72.1 us
    psum x1, blocking collectives, per_device(): col_total = lax.psum(jnp.sum(squares, axis=0), ('dp', 'seq'))  70.6 us
    all_gather x1, waiting for transfers between devices, per_device(): new_weight = lax.all_gather(fresh, 'seq', axis=0, tiled=True)  50.3 us
    unnamed x1, blocking collectives  13.9 us
    dot_general x1, matrix products, per_device(): lax.dot_general(hidden, grad_out, (((0,), (0,)), ((), ())), preferred_ele...  10.5 us
  transfers between devices with their start and end apart: 2, of which 2 were waited for; matrix products, arithmetic and copies ran while one was open for 0% of the time, Pallas kernels for 0%

profile of v1, /device:TPU:1, one launch (start us, length us, event | category | flops | bytes accessed | tf_op | source)
XLA Modules:
  0.0 363.0 jit_solution(14424026349936314652)
XLA Ops:
  7.2 0.0 copy-start
  7.2 0.0 reduce-scatter.2.cloned.1.call-start
  7.2 1.0 copy-done
  8.2 10.5 %fusion.4 = f32[7168,512]{1,0:T(8,128)} fusion(bf16[512,7168]{1,0:T(8,128)(2,1)} %param.5, bf16[512,512]{1,0:T(8,128)(2,1)S(1)} %copy-done), kind=kOutput, calls=%fused_computation.9 | convolution fusion | flops 3758096384 | bytes 22544384 | tf_op jit(solution)/shard_map/dot_general | solution.py:15
  18.7 0.0 copy-start.6
  18.7 0.0 copy-start.5
  18.7 0.0 copy-start.4
  18.7 0.0 copy-start.1
  18.7 0.0 reduce-scatter.2.cloned.1.call-update
  18.7 0.0 all-gather.3.cloned.1.call-start
  18.8 0.6 copy-done.6
  19.4 0.6 dynamic-slice
  20.6 118.3 %reduce-scatter.2.cloned.1.call-done = f32[224,512]{1,0:T(8,128)} async-done(((f32[7168,512]{1,0:T(8,128)}), f32[224,512]{1,0:T(8,128)}) %reduce-scatter.2.cloned.1.call-update) | async-done | bytes 458768 | tf_op jit(solution)/shard_map/reduce_scatter | solution.py:14
  138.9 1.2 fusion.1
  140.1 0.3 dynamic-update-slice
  140.3 13.9 %all-reduce = f32[1792]{0:T(1024)S(1)} all-reduce(f32[1792]{0:T(1024)S(1)} %dynamic-update-slice), channel_id=2, replica_groups=mesh['dp'=2,'seq'=16,'tensor'=8] {'tensor'}, use_global_device_ids=true, to_apply=%add | all-reduce | flops 1792 | bytes 14336
  154.2 0.1 reshape.10
  154.3 70.6 %psum.14 = f32[512]{0:T(512)S(1)} all-reduce(f32[512]{0:T(512)S(1)} %get-tuple-element.5), channel_id=1, replica_groups=mesh['dp'=2,'seq'=16,'tensor'=8] {'dp','seq'}, use_global_device_ids=true, to_apply=%region_4.0 | all-reduce | flops 512 | bytes 4096 | tf_op jit(solution)/shard_map/psum | solution.py:23
  224.9 0.0 copy-done.5
  225.0 0.0 copy-done.4
  225.0 0.0 copy-start.3
  225.0 0.0 copy-start.2
  225.0 1.8 multiply_reduce_fusion
  226.8 72.1 %psum.15 = f32[]{:T(128)} all-reduce(f32[]{:T(128)} %multiply_reduce_fusion), channel_id=1, replica_groups=mesh['dp'=2,'seq'=16,'tensor'=8] {'dp','seq','tensor'}, use_global_device_ids=true, to_apply=%region_6.0 | all-reduce | flops 1 | bytes 8 | tf_op jit(solution)/shard_map/psum | solution.py:31
  299.6 0.0 copy-done.1
  299.6 2.0 subtract_convert_fusion
  301.7 0.0 all-gather.3.cloned.1.call-update
  301.7 50.3 %all-gather.3.cloned.1.call-done = bf16[3584,512]{1,0:T(8,128)(2,1)} async-done(((bf16[224,512]{1,0:T(8,128)(2,1)}), bf16[3584,512]{1,0:T(8,128)(2,1)}) %all-gather.3.cloned.1.call-update) | async-done | bytes 3670032 | tf_op jit(solution)/shard_map/all_gather | solution.py:35
  352.0 4.1 %copy.11 = bf16[3584,512]{1,0:T(8,128)(2,1)} copy(bf16[3584,512]{1,0:T(8,128)(2,1)} %all-gather.3.cloned.1.call-done) | data formatting | bytes 7340032
  356.1 0.0 copy-done.3
  356.1 0.0 copy-done.2
  (4 shorter events, 0.0 us)
Async XLA Ops:
  7.2 1.0 copy-start
  7.2 131.7 %reduce-scatter.2.cloned.1.call-start = ((), (), s32[]{:S(2)}) async-start(), calls=%async_computation.1 | async-start | bytes 15138816 | tf_op jit(solution)/shard_map/reduce_scatter | solution.py:14
  18.7 0.7 copy-start.6
  18.7 206.2 %copy-start.5 = (f32[224]{0:T(256)S(1)}, f32[224]{0:T(256)}, u32[]{:S(2)}) copy-start(f32[224]{0:T(256)} %param.8) | copy-start | bytes 2692
  18.7 206.3 %copy-start.4 = (f32[512]{0:T(512)S(1)}, f32[512]{0:T(512)}, u32[]{:S(2)}) copy-start(f32[512]{0:T(512)} %param.9) | copy-start | bytes 6148
  18.7 280.9 %copy-start.1 = (f32[224,512]{1,0:T(8,128)S(1)}, f32[224,512]{1,0:T(8,128)}, u32[]{:S(2)}) copy-start(f32[224,512]{1,0:T(8,128)} %param.7) | copy-start | bytes 1376260
  18.7 333.3 %all-gather.3.cloned.1.call-start = ((), (), s32[]{:S(2)}) async-start(), calls=%async_computation.2 | async-start | bytes 3899392 | tf_op jit(solution)/shard_map/all_gather | solution.py:35
  225.0 131.2 %copy-start.3 = (f32[224]{0:T(256)}, f32[224]{0:T(256)S(1)}, u32[]{:S(2)}) copy-start(f32[224]{0:T(256)S(1)} %multiply_add_fusion.2) | copy-start | bytes 2692
  225.0 131.2 %copy-start.2 = (f32[512]{0:T(512)}, f32[512]{0:T(512)S(1)}, u32[]{:S(2)}) copy-start(f32[512]{0:T(512)S(1)} %multiply_add_fusion.1) | copy-start | bytes 6148
Sparse Core Ops, SparseCore 0:
  18.9 119.9 reduce-scatter.1
  301.8 50.1 all-gather.2

commit v2 on v0

--- a/solution.py
+++ b/solution.py
@@ -11,6 +11,11 @@
 
 
 def per_device(hidden, grad_out, master_weight, row_prev, col_prev):
+
+    def start_screen(x0, mesh_name, across):
+        tall = lax.psum(x0, mesh_name)
+        return lax.psum(tall, across)
+
     grads = lax.psum_scatter(
         lax.dot_general(
             hidden, grad_out, (((0,), (0,)), ((), ())), preferred_element_type=jnp.float32
@@ -20,7 +25,7 @@
         tiled=True,
     )
     squares = grads * grads + small_term
-    col_total = lax.psum(jnp.sum(squares, axis=0), ("dp", "seq"))
+    col_total = start_screen(jnp.sum(squares, axis=0), "seq", "dp")
     row_total = lax.psum(jnp.sum(squares, axis=1), "tensor")
     new_rows = decay_rate * row_prev + (1.0 - decay_rate) * row_total / D
     new_cols = decay_rate * col_prev + (1.0 - decay_rate) * col_total / FF_WIN

time: 363 us -> 339 us (0.934)
  blocking collectives: 156 us -> 132 us
    psum x1 -> x2, blocking collectives: 70.5 us -> 45.8 us  [the longest x1 30.9 us: start_screen(): tall = lax.psum(x0, mesh_name)]
where the time goes in v2:
time: 339 us; the launch traced here: 338 us
  waiting for transfers between devices  170 us (50%)
  blocking collectives  132 us (39%)
  between operations  14.8 us (4%)
  matrix products  10.5 us (3%)
  local copies, waits for them, and re-layouts  5.13 us (2%)
  other arithmetic  5.03 us (1%)
    reduce_scatter x1, waiting for transfers between devices, per_device(): lax.psum_scatter(lax.dot_general(hidden, grad_out, (((0,), (0,)), ((), ()...  120 us
    psum x1, blocking collectives, per_device(): raw_total = lax.psum(jnp.sum(raw * raw), ('dp', 'seq', 'tensor'))  72.7 us
    all_gather x1, waiting for transfers between devices, per_device(): new_weight = lax.all_gather(fresh, 'seq', axis=0, tiled=True)  50.3 us
    psum x1, blocking collectives, start_screen(): tall = lax.psum(x0, mesh_name)  30.9 us
    psum x1, blocking collectives, start_screen(): return lax.psum(tall, across)  14.9 us
    psum x1, blocking collectives, per_device(): row_total = lax.psum(jnp.sum(squares, axis=1), 'tensor')  13.7 us
    dot_general x1, matrix products, per_device(): lax.dot_general(hidden, grad_out, (((0,), (0,)), ((), ())), preferred_ele...  10.5 us
  transfers between devices with their start and end apart: 2, of which 2 were waited for; matrix products, arithmetic and copies ran while one was open for 0% of the time, Pallas kernels for 0%

profile of v2, /device:TPU:1, one launch (start us, length us, event | category | flops | bytes accessed | tf_op | source)
XLA Modules:
  0.0 338.2 jit_solution(11403570304043887320)
XLA Ops:
  7.2 0.0 copy-start
  7.2 0.0 reduce-scatter.2.cloned.1.call-start
  7.2 1.0 copy-done
  8.2 10.5 %fusion.4 = f32[7168,512]{1,0:T(8,128)} fusion(bf16[512,7168]{1,0:T(8,128)(2,1)} %param.5, bf16[512,512]{1,0:T(8,128)(2,1)S(1)} %copy-done), kind=kOutput, calls=%fused_computation.9 | convolution fusion | flops 3758096384 | bytes 22544384 | tf_op jit(solution)/shard_map/dot_general | solution.py:20
  18.7 0.0 copy-start.5
  18.7 0.0 copy-start.4
  18.7 0.0 copy-start.1
  18.7 0.0 reduce-scatter.2.cloned.1.call-update
  18.7 0.0 all-gather.2.cloned.1.call-start
  18.8 120.1 %reduce-scatter.2.cloned.1.call-done = f32[224,512]{1,0:T(8,128)} async-done(((f32[7168,512]{1,0:T(8,128)}), f32[224,512]{1,0:T(8,128)}) %reduce-scatter.2.cloned.1.call-update) | async-done | bytes 458768 | tf_op jit(solution)/shard_map/reduce_scatter | solution.py:19
  138.9 1.2 fusion.1
  140.0 13.7 %psum.28 = f32[224]{0:T(256)S(1)} all-reduce(f32[224]{0:T(256)S(1)} %get-tuple-element.4), channel_id=1, replica_groups=mesh['dp'=2,'seq'=16,'tensor'=8] {'tensor'}, use_global_device_ids=true, to_apply=%region_2.0 | all-reduce | flops 224 | bytes 1792 | tf_op jit(solution)/shard_map/psum | solution.py:29
  153.8 30.9 %psum.29 = f32[512]{0:T(512)S(1)} all-reduce(f32[512]{0:T(512)S(1)} %get-tuple-element.5), channel_id=1, replica_groups=mesh['dp'=2,'seq'=16,'tensor'=8] {'seq'}, use_global_device_ids=true, to_apply=%region_4.0 | all-reduce | flops 512 | bytes 4096 | tf_op jit(solution)/shard_map/psum | solution.py:16
  184.7 14.9 %psum.30 = f32[512]{0:T(512)S(1)} all-reduce(f32[512]{0:T(512)S(1)} %psum.29), channel_id=1, replica_groups=mesh['dp'=2,'seq'=16,'tensor'=8] {'dp'}, use_global_device_ids=true, to_apply=%region_5.0 | all-reduce | flops 512 | bytes 4096 | tf_op jit(solution)/shard_map/psum | solution.py:17
  199.6 0.0 copy-done.5
  199.6 0.0 copy-done.4
  199.6 0.0 copy-start.3
  199.7 0.0 copy-start.2
  199.7 1.8 multiply_reduce_fusion
  201.5 72.7 %psum.31 = f32[]{:T(128)} all-reduce(f32[]{:T(128)} %multiply_reduce_fusion), channel_id=1, replica_groups=mesh['dp'=2,'seq'=16,'tensor'=8] {'dp','seq','tensor'}, use_global_device_ids=true, to_apply=%region_7.0 | all-reduce | flops 1 | bytes 8 | tf_op jit(solution)/shard_map/psum | solution.py:34
  274.9 0.0 copy-done.1
  274.9 2.0 subtract_convert_fusion
  276.9 0.0 all-gather.2.cloned.1.call-update
  276.9 50.3 %all-gather.2.cloned.1.call-done = bf16[3584,512]{1,0:T(8,128)(2,1)} async-done(((bf16[224,512]{1,0:T(8,128)(2,1)}), bf16[3584,512]{1,0:T(8,128)(2,1)}) %all-gather.2.cloned.1.call-update) | async-done | bytes 3670032 | tf_op jit(solution)/shard_map/all_gather | solution.py:38
  327.2 4.1 %copy.10 = bf16[3584,512]{1,0:T(8,128)(2,1)} copy(bf16[3584,512]{1,0:T(8,128)(2,1)} %all-gather.2.cloned.1.call-done) | data formatting | bytes 7340032
  331.3 0.0 copy-done.3
  331.3 0.0 copy-done.2
  (2 shorter events, 0.0 us)
Async XLA Ops:
  7.2 1.0 copy-start
  7.2 131.7 %reduce-scatter.2.cloned.1.call-start = ((), (), s32[]{:S(2)}) async-start(), calls=%async_computation.1 | async-start | bytes 15138816 | tf_op jit(solution)/shard_map/reduce_scatter | solution.py:19
  18.7 180.9 %copy-start.5 = (f32[224]{0:T(256)S(1)}, f32[224]{0:T(256)}, u32[]{:S(2)}) copy-start(f32[224]{0:T(256)} %param.8) | copy-start | bytes 2692
  18.7 180.9 %copy-start.4 = (f32[512]{0:T(512)S(1)}, f32[512]{0:T(512)}, u32[]{:S(2)}) copy-start(f32[512]{0:T(512)} %param.9) | copy-start | bytes 6148
  18.7 256.2 %copy-start.1 = (f32[224,512]{1,0:T(8,128)S(1)}, f32[224,512]{1,0:T(8,128)}, u32[]{:S(2)}) copy-start(f32[224,512]{1,0:T(8,128)} %param.7) | copy-start | bytes 1376260
  18.7 308.5 %all-gather.2.cloned.1.call-start = ((), (), s32[]{:S(2)}) async-start(), calls=%async_computation.2 | async-start | bytes 3899392 | tf_op jit(solution)/shard_map/all_gather | solution.py:38
  199.6 131.7 %copy-start.3 = (f32[224]{0:T(256)}, f32[224]{0:T(256)S(1)}, u32[]{:S(2)}) copy-start(f32[224]{0:T(256)S(1)} %multiply_add_fusion.2) | copy-start | bytes 2692
  199.7 131.7 %copy-start.2 = (f32[512]{0:T(512)}, f32[512]{0:T(512)S(1)}, u32[]{:S(2)}) copy-start(f32[512]{0:T(512)S(1)} %multiply_add_fusion.1) | copy-start | bytes 6148
Sparse Core Ops, SparseCore 0:
  18.8 119.9 reduce-scatter.1
  277.0 50.1 all-gather.1
